TPU v7x, 32 devices: a whole 2x2x4 slice. The times are simulated.
32 devices in a mesh: ens: 4 (over x, core), space: 8 (over z, y).
Axes of the slice: x: 2, y: 2, z: 4, core: 2. Of those that a mesh axis runs over, the one named last changes fastest.
Arguments:
- latents: bfloat16 [8, 32, 256, 256], P('ens', None, 'space'), may hold values from -6 to 6
- targets: bfloat16 [32, 256, 256], P(None, 'space'), may hold values from -6 to 6
- kernel: bfloat16 [3, 3, 256, 256], replicated, may hold values from -0.125 to 0.125
Outputs:
- loss: float32 [], replicated
- grad_input: bfloat16 [8, 32, 256, 256], P('ens', None, 'space')
- grad_kernel: float32 [3, 3, 256, 256], replicated
All inputs are finite; a program needn't handle non-finite values.
Results may differ from a plain program's by a relative error of at most 0.0047.
Values may be sent and summed in bfloat16 or wider, within the bound.
A program may use at most 64 MiB of HBM per device.

v0:
```python
import jax
import jax.numpy as jnp
from jax import lax
from jax.sharding import PartitionSpec as P

smoothing = 0.1


def padded_2(block, sides, width):
    for axis, dim in sides:
        count = lax.axis_size(axis)
        forward = [(i, i + 1) for i in range(count - 1)]
        forward.append((count - 1, 0))
        backward = [(target, source) for source, target in forward]
        low = lax.ppermute(
            lax.slice_in_dim(block, block.shape[dim] - width, None, axis=dim), axis, forward
        )
        high = lax.ppermute(lax.slice_in_dim(block, 0, width, axis=dim), axis, backward)
        block = jnp.concatenate([low, block, high], axis=dim)
    return block


def lat_pad(field):
    return jnp.pad(field, ((0, 0), (1, 1), (0, 0), (0, 0)))


def conv_forward(padded, kernel, rows, cols):
    chans = padded.shape[3]
    total = None
    for row_off in range(3):
        for col_off in range(3):
            window = padded[:, row_off : row_off + rows, col_off : col_off + cols, :].reshape(
                -1, chans
            )
            term = jnp.dot(window, kernel[row_off, col_off], preferred_element_type=jnp.float32)
            total = term if total is None else total + term
    return total.reshape(padded.shape[0], rows, cols, -1)


def conv_adjoint(padded, kernel, rows, cols):
    chans = padded.shape[3]
    total = None
    for row_off in range(3):
        for col_off in range(3):
            window = padded[
                :, 2 - row_off : 2 - row_off + rows, 2 - col_off : 2 - col_off + cols, :
            ].reshape(-1, chans)
            term = lax.dot_general(
                window,
                kernel[row_off, col_off],
                (((1,), (1,)), ((), ())),
                preferred_element_type=jnp.float32,
            )
            total = term if total is None else total + term
    return total.reshape(padded.shape[0], rows, cols, -1)


def kernel_terms(padded, slopes, rows, cols):
    chans = padded.shape[3]
    flat_slopes = slopes.reshape(-1, slopes.shape[3])
    blocks = []
    for row_off in range(3):
        for col_off in range(3):
            window = padded[:, row_off : row_off + rows, col_off : col_off + cols, :].reshape(
                -1, chans
            )
            blocks.append(
                lax.dot_general(
                    window,
                    flat_slopes,
                    (((0,), (0,)), ((), ())),
                    preferred_element_type=jnp.float32,
                )
            )
    return jnp.stack(blocks).reshape(3, 3, chans, -1)


def local(latents, targets, kernel):
    members_dev, rows, cols, chans = latents.shape
    members = members_dev * lax.axis_size("ens")
    longitude = cols * lax.axis_size("space")
    rimmed = padded_2(latents, (("space", 2),), 1)
    padded = lat_pad(rimmed)
    fields = conv_forward(padded, kernel, rows, cols)
    offset = fields - targets.astype(jnp.float32)[None]
    spread = jnp.sqrt(offset * offset + smoothing * smoothing)
    own_total = jnp.sum(spread)
    own_slope = offset / spread
    block = lax.all_to_all(fields, "ens", split_axis=1, concat_axis=0, tiled=True)
    gap = block[:, None] - block[None]
    width = jnp.sqrt(gap * gap + smoothing * smoothing)
    slope = jnp.sum(gap / width, axis=1)
    returned = lax.all_to_all(slope, "ens", split_axis=0, concat_axis=1, tiled=True)
    part_total = jnp.sum(width, axis=(0, 1))[None] - block.shape[0] * smoothing
    pair_total = jnp.sum(part_total)
    slopes = (own_slope / members - returned / (members * (members - 1))).astype(jnp.bfloat16)
    cell_sum = own_total / members - pair_total / (2 * members * (members - 1))
    slope_rimmed = padded_2(slopes, (("space", 2),), 1)
    grad_input = conv_adjoint(lat_pad(slope_rimmed), kernel, rows, cols).astype(jnp.bfloat16)
    partial_kernel = kernel_terms(padded, slopes, rows, cols) / (members * rows * longitude)
    grad_kernel, loss_total = lax.psum((partial_kernel, cell_sum), ("ens", "space"))
    loss = loss_total / (rows * longitude * chans)
    return (loss, grad_input, grad_kernel)


def solution(mesh):
    in_specs = (P("ens", None, "space", None), P(None, "space", None), P())
    out_specs = (P(), P("ens", None, "space", None), P())
    return jax.shard_map(local, mesh=mesh, in_specs=in_specs, out_specs=out_specs, check_vma=False)
```

profile of v0, /device:TPU:1, one launch (start us, length us, event | category | flops | bytes accessed | tf_op | source)
XLA Modules:
  0.0 299.6 jit_solution(1788002785526001829)
XLA Ops:
  7.2 1.2 fusion.72
  8.4 2.1 collective-permute-start
  10.5 3.1 %collective-permute-start.1 = (bf16[2,32,1,256]{3,2,1,0:T(2,128)(2,1)S(1)}, bf16[2,32,1,256]{3,2,1,0:T(2,128)(2,1)S(1)}, u32[]{:S(2)}, u32[]{:S(2)}) collective-permute-start(bf16[2,32,1,256]{3,2,1,0:T(2,128)(2,1)S(1)} %get-tuple-element.26), channel_id=1, source_target_pairs={{1,0},{2,1},{3,2},{4,3},{5,4},{6,5},{7,6},{0,7},{9,8},{10,9},{11,1... | collective-permute-start | bytes 98312 | tf_op jit(solution)/shard_map/ppermute | solution.py:18
  13.6 1.6 fusion.33
  15.3 0.8 select_maximum_fusion.2
  16.2 1.0 fusion.70
  18.3 0.4 convolution_add_fusion.11
  19.2 1.2 pad_maximum_fusion.2
  20.8 0.5 copy-done.5
  23.2 29.0 %all_to_all.24 = f32[2,32,32,256]{3,2,0,1:T(8,128)S(1)} all-to-all(f32[2,32,32,256]{3,2,0,1:T(8,128)S(1)} %copy.19), channel_id=1, replica_groups=mesh['ens'=4,'space'=8] {'ens'}, dimensions={1} | all-to-all | bytes 4194304 | tf_op jit(solution)/shard_map/all_to_all | solution.py:89
  52.4 9.9 %fusion.3 = (f32[8,8,32,256]{3,2,1,0:T(8,128)}, f32[8,32,256]{2,1,0:T(8,128)}) fusion(f32[8,8,32,256]{3,2,1,0:T(8,128)S(1)} %bitcast.208), kind=kLoop, calls=%fused_computation.5 | loop fusion | flops 24576000 | bytes 4456448 | tf_op jit(solution)/shard_map/reduce_sum | solution.py:92
  62.4 5.4 %all-to-all-start.1 = ((f32[8,8,32,256]{3,2,1,0:T(8,128)}), f32[8,8,32,256]{3,2,1,0:T(8,128)}, u32[]{:S(2)}, u32[]{:S(2)}) async-start(f32[8,8,32,256]{3,2,1,0:T(8,128)} %get-tuple-element.3), calls=%async_computation.1 | async-start | bytes 4194304 | tf_op jit(solution)/shard_map/all_to_all | solution.py:93
  67.8 2.1 convert_element_type.18
  70.0 1.6 add_reduce_fusion
  72.2 20.5 %all-to-all-done.1 = f32[8,8,32,256]{3,2,1,0:T(8,128)} async-done(((f32[8,8,32,256]{3,2,1,0:T(8,128)}), f32[8,8,32,256]{3,2,1,0:T(8,128)}, u32[]{:S(2)}, u32[]{:S(2)}) %all-to-all-start.1) | async-done | bytes 2097184 | tf_op jit(solution)/shard_map/all_to_all | solution.py:93
  92.8 1.8 broadcast_multiply_fusion.1
  94.8 1.0 copy-done.7
  95.8 2.8 fusion.10
  98.6 2.3 subtract_convert_fusion
  100.8 0.8 fusion.71
  101.6 0.5 fusion.20
  102.0 0.8 collective-permute-start.2
  102.8 3.6 %collective-permute-start.3 = (bf16[2,32,1,256]{3,2,1,0:T(2,128)(2,1)}, bf16[2,32,1,256]{3,2,1,0:T(2,128)(2,1)}, u32[]{:S(2)}, u32[]{:S(2)}) collective-permute-start(bf16[2,32,1,256]{3,2,1,0:T(2,128)(2,1)} %get-tuple-element.22), channel_id=1, source_target_pairs={{1,0},{2,1},{3,2},{4,3},{5,4},{6,5},{7,6},{0,7},{9,8},{10,9},{11,1... | collective-permute-start | bytes 98312 | tf_op jit(solution)/shard_map/ppermute | solution.py:18
  106.4 0.5 fusion.19
  106.9 0.5 fusion.18
  107.4 0.7 copy-done.6
  108.1 0.5 fusion.17
  108.6 0.5 fusion.16
  109.4 0.5 fusion.15
  109.9 0.5 fusion.14
  110.4 0.5 fusion.13
  110.9 0.5 fusion.12
  111.4 1.6 broadcast_multiply_fusion
  113.8 1.8 fusion.31
  115.6 37.0 %psum.14 = f32[]{:T(128)} all-reduce(f32[]{:T(128)S(6)} %sub.50), channel_id=1, replica_groups=mesh['ens'=4,'space'=8] {'ens','space'}, use_global_device_ids=true, to_apply=%region_3.4 | all-reduce | flops 1 | bytes 8 | tf_op jit(solution)/shard_map/psum | solution.py:101
  153.3 1.7 select_maximum_fusion
  155.0 1.0 fusion.69
  156.0 0.5 fusion.41
  156.5 0.5 convolution_add_fusion.5
  156.9 0.5 convolution_add_fusion.4
  157.4 2.1 pad_maximum_fusion
  159.5 0.5 fusion.6
  160.0 0.5 fusion.25
  160.5 0.5 fusion.5
  160.9 0.5 convolution_add_fusion.1
  161.4 1.4 fusion.9
  162.9 125.5 %all-reduce.4.cloned.1.call-done = f32[3,3,256,256]{3,2,1,0:T(8,128)} async-done(((f32[3,3,256,256]{3,2,1,0:T(8,128)}), f32[3,3,256,256]{3,2,1,0:T(8,128)}) %all-reduce.4.cloned.1.call-update) | async-done | bytes 2359312 | tf_op jit(solution)/shard_map/psum | solution.py:101
  288.4 3.2 %copy.45 = f32[3,3,256,256]{3,2,1,0:T(8,128)} copy(f32[3,3,256,256]{3,2,1,0:T(8,128)} %all-reduce.4.cloned.1.call-done) | data formatting | bytes 4718592
  (37 shorter events, 4.8 us)
Async XLA Ops:
  7.2 8.2 %copy-start.1 = (bf16[2,32,32,256]{3,2,1,0:T(8,128)(2,1)S(1)}, bf16[2,32,32,256]{3,2,1,0:T(8,128)(2,1)}, u32[]{:S(2)}) copy-start(bf16[2,32,32,256]{3,2,1,0:T(8,128)(2,1)} %param.3) | copy-start | bytes 3145732
  8.4 6.9 %collective-permute-start = (bf16[2,32,1,256]{3,2,1,0:T(2,128)(2,1)S(1)}, bf16[2,32,1,256]{3,2,1,0:T(2,128)(2,1)S(1)}, u32[]{:S(2)}, u32[]{:S(2)}) collective-permute-start(bf16[2,32,1,256]{3,2,1,0:T(2,128)(2,1)S(1)} %get-tuple-element.25), channel_id=1, source_target_pairs={{0,1},{1,2},{2,3},{3,4},{4,5},{5,6},{6,7},{7,0},{8,9},{9,10},{10,1... | collective-permute-start | bytes 98312 | tf_op jit(solution)/shard_map/ppermute | solution.py:15
  10.5 4.8 %collective-permute-start.1 = (bf16[2,32,1,256]{3,2,1,0:T(2,128)(2,1)S(1)}, bf16[2,32,1,256]{3,2,1,0:T(2,128)(2,1)S(1)}, u32[]{:S(2)}, u32[]{:S(2)}) collective-permute-start(bf16[2,32,1,256]{3,2,1,0:T(2,128)(2,1)S(1)} %get-tuple-element.26), channel_id=1, source_target_pairs={{1,0},{2,1},{3,2},{4,3},{5,4},{6,5},{7,6},{0,7},{9,8},{10,9},{11,1... | collective-permute-start | bytes 98312 | tf_op jit(solution)/shard_map/ppermute | solution.py:18
  16.2 1.3 copy-start.9
  20.4 1.0 copy-start.5
  20.4 1.3 copy-start.3
  23.0 71.8 %copy-start = (f32[2048,256]{1,0:T(8,128)}, f32[2048,256]{1,0:T(8,128)S(1)}, u32[]{:S(2)}) copy-start(f32[2048,256]{1,0:T(8,128)S(1)} %convolution_add_fusion.6) | copy-start | bytes 6291460
  62.4 30.4 %all-to-all-start.1 = ((f32[8,8,32,256]{3,2,1,0:T(8,128)}), f32[8,8,32,256]{3,2,1,0:T(8,128)}, u32[]{:S(2)}, u32[]{:S(2)}) async-start(f32[8,8,32,256]{3,2,1,0:T(8,128)} %get-tuple-element.3), calls=%async_computation.1 | async-start | bytes 4194304 | tf_op jit(solution)/shard_map/all_to_all | solution.py:93
  67.8 220.6 %all-reduce.4.cloned.1.call-start = ((), (), s32[]{:S(2)}) async-start(), calls=%async_computation.2 | async-start | bytes 4718592 | tf_op jit(solution)/shard_map/psum | solution.py:101
  94.6 1.2 copy-start.7
  102.0 51.3 %collective-permute-start.2 = (bf16[2,32,1,256]{3,2,1,0:T(2,128)(2,1)}, bf16[2,32,1,256]{3,2,1,0:T(2,128)(2,1)S(1)}, u32[]{:S(2)}, u32[]{:S(2)}) collective-permute-start(bf16[2,32,1,256]{3,2,1,0:T(2,128)(2,1)} %get-tuple-element.21), channel_id=1, source_target_pairs={{0,1},{1,2},{2,3},{3,4},{4,5},{5,6},{6,7},{7,0},{8,9},{9,10},{10,1... | collective-permute-start | bytes 98312 | tf_op jit(solution)/shard_map/ppermute | solution.py:15
  102.8 50.5 %collective-permute-start.3 = (bf16[2,32,1,256]{3,2,1,0:T(2,128)(2,1)}, bf16[2,32,1,256]{3,2,1,0:T(2,128)(2,1)}, u32[]{:S(2)}, u32[]{:S(2)}) collective-permute-start(bf16[2,32,1,256]{3,2,1,0:T(2,128)(2,1)} %get-tuple-element.22), channel_id=1, source_target_pairs={{1,0},{2,1},{3,2},{4,3},{5,4},{6,5},{7,6},{0,7},{9,8},{10,9},{11,1... | collective-permute-start | bytes 98312 | tf_op jit(solution)/shard_map/ppermute | solution.py:18
  106.9 1.2 copy-start.6
  106.9 1.7 copy-start.2
  108.1 1.3 copy-start.4
  111.4 2.3 copy-start.10
  111.4 2.4 copy-start.11
  157.4 2.1 copy-start.8
Sparse Core Ops, SparseCore 0:
  152.8 135.5 all-reduce.3
where the time goes:
time: 302 us; the launch traced here: 300 us
  waiting for transfers between devices  146 us (48%)
  blocking collectives  66.1 us (22%)
  other arithmetic  27.9 us (9%)
  between operations  17.5 us (6%)
  matrix products  16 us (5%)
  starting transfers between devices  15 us (5%)
  local copies, waits for them, and re-layouts  11.1 us (4%)
    psum x1, waiting for transfers between devices, local(): lax.psum((partial_kernel, cell_sum), ('ens', 'space'))  126 us
    psum x1, blocking collectives, local(): lax.psum((partial_kernel, cell_sum), ('ens', 'space'))  37 us
    all_to_all x1, blocking collectives, local(): lax.all_to_all(fields, 'ens', split_axis=1, concat_axis=0, tiled=True)  29 us
    all_to_all x1, waiting for transfers between devices, local(): lax.all_to_all(slope, 'ens', split_axis=0, concat_axis=1, tiled=True)  20.5 us
    reduce_sum x1, other arithmetic, local(): slope = jnp.sum(gap / width, axis=1)  9.94 us
    ppermute x2, starting transfers between devices, padded_2(): lax.ppermute(lax.slice_in_dim(block, 0, width, axis=dim), axis, backward)  6.66 us
    unnamed x25, local copies, waits for them, and re-layouts  6.52 us
    dot_general x9, matrix products, conv_adjoint(): lax.dot_general(window, kernel[row_off, col_off], (((1,), (1,)), ((), ())...  6.49 us
  transfers between devices with their start and end apart: 6, of which 2 were waited for; matrix products, arithmetic and copies ran while one was open for 7% of the time, Pallas kernels for 0%

commit v1 on v0

v1 whole, which is shorter than its diff:
```python
import functools

import jax
import jax.numpy as jnp
from jax import lax
from jax.experimental import pallas as pl
from jax.experimental.pallas import tpu as pltpu
from jax.sharding import PartitionSpec as P

smoothing = 0.1
WIRE = jnp.bfloat16
ROW_CHUNK = 4
F32, BF16 = jnp.float32, jnp.bfloat16
NT = (((1,), (1,)), ((), ()))


def rim(block, count):
    cols = block.shape[2]
    forward = [(i, (i + 1) % count) for i in range(count)]
    backward = [(t, s) for s, t in forward]
    low = lax.ppermute(block[:, :, cols - 1 :], "space", forward)
    high = lax.ppermute(block[:, :, :1], "space", backward)
    left = jnp.concatenate([low, block[:, :, : cols - 1]], axis=2)
    right = jnp.concatenate([block[:, :, 1:], high], axis=2)
    return jnp.pad(jnp.stack([left, block, right]), ((0, 0), (0, 0), (1, 1), (0, 0), (0, 0)))


def body(
    n, members,
    x_ref, t_ref, k_ref,
    gi_ref, gk_ref, loss_ref,
    f_own, own, co, xp, xc, sp, acc, eo, ei, r1, b2, r2, b3, r3, l1, lr1, l2, lr2, l3, lr3,
    s_x, r_x, s_c, r_c, s_l, r_l, s_e, r_e, s_st, r_st, s_ls, r_ls, s_sp, r_sp, s_lp, r_lp,
    s_ag, r_ag,
):
    mdev, rows, cols, chans = gi_ref.shape
    rc = ROW_CHUNK
    chunks = rows // rc
    cells = rc * cols
    part = b3.shape[0] // n
    e = lax.axis_index("ens")
    s = lax.axis_index("space")
    core = lax.rem(e, 2)
    xx = e // 2
    cpeer = {"ens": xx * 2 + (1 - core)}
    xpeer = {"ens": (1 - xx) * 2 + core}
    right = {"space": lax.rem(s + 1, n)}
    left = {"space": lax.rem(s + n - 1, n)}

    def rcopy(src, dst, ss, rs, dev):
        return pltpu.make_async_remote_copy(
            src_ref=src, dst_ref=dst, send_sem=ss, recv_sem=rs,
            device_id=dev, device_id_type=pl.DeviceIdType.MESH,
        )

    barrier = pltpu.get_barrier_semaphore()
    for dev in (cpeer, xpeer):
        pl.semaphore_signal(barrier, inc=1, device_id=dev, device_id_type=pl.DeviceIdType.MESH)

    @pl.loop(1, n)
    def _(d):
        pl.semaphore_signal(
            barrier, inc=1, device_id={"space": lax.rem(s + d, n)},
            device_id_type=pl.DeviceIdType.MESH,
        )

    pl.semaphore_wait(barrier, n + 1)

    def to_x(ch):
        return rcopy(own.at[ch], xp.at[ch], s_x.at[ch], r_x.at[ch], xpeer)

    def to_core(ch):
        return rcopy(own.at[ch], co.at[ch], s_c.at[ch], r_c.at[ch], cpeer)

    def relay(ch):
        return rcopy(xp.at[ch], xc.at[ch], s_l.at[ch], r_l.at[ch], cpeer)

    @pl.loop(0, chunks)
    def _(ch):
        total = None
        for a in range(3):
            for b in range(3):
                w = x_ref[b, :, pl.ds(ch * rc + a, rc)].reshape(mdev * cells, chans)
                term = jnp.dot(w, k_ref[a * 3 + b], preferred_element_type=F32)
                total = term if total is None else total + term
        total = total.reshape(mdev, cells, chans)
        f_own[ch] = total
        own[ch] = total.astype(WIRE)
        to_x(ch).start()
        to_core(ch).start()

    acc[...] = jnp.zeros_like(acc)
    loss_ref[...] = jnp.zeros_like(loss_ref)
    for c in range(3):
        for r in (0, rows + 1):
            sp[c, :, r] = jnp.zeros((mdev, cols, chans), BF16)

    def smooth(gap):
        square = gap * gap + smoothing * smoothing
        inv = lax.rsqrt(square)
        return gap * inv, square * inv

    def process(ch):
        @pl.loop(0, rc)
        def _(q):
            row = ch * rc + q
            for blk in range(cols // 16):
                at = pl.ds(pl.multiple_of(q * cols + blk * 16, 16), 16)
                mine = [f_own[ch, m, at] for m in range(mdev)]
                tgt = t_ref[row, pl.ds(blk * 16, 16)].astype(F32)
                slopes, own_w, pair_w = [], None, None
                own_s = []
                for f in mine:
                    sl, w = smooth(f - tgt)
                    own_s.append(sl)
                    own_w = w if own_w is None else own_w + w
                sl, w = smooth(mine[0] - mine[1])
                sums = [sl, -sl]
                pair_w = w + w
                for ref in (co, xp, xc):
                    for m in range(mdev):
                        o = ref[ch, m, at].astype(F32)
                        for k in range(mdev):
                            sl, w = smooth(mine[k] - o)
                            sums[k] = sums[k] + sl
                            pair_w = pair_w + w
                loss_ref[...] += own_w * (1.0 / members) - pair_w * (
                    1.0 / (2 * members * (members - 1))
                )
                for m in range(mdev):
                    sl = own_s[m] * (1.0 / members) - sums[m] * (1.0 / (members * (members - 1)))
                    sp[1, m, 1 + row, pl.ds(blk * 16, 16)] = sl.astype(BF16)
                    if blk == 0:
                        eo[0, pl.ds(m * rows + row, 1)] = sl[0:1]
                    if blk == cols // 16 - 1:
                        eo[1, pl.ds(m * rows + row, 1)] = sl[15:16]

        sl = sp[1, :, pl.ds(1 + ch * rc, rc)].reshape(mdev * cells, chans)
        slt = sl.astype(F32).T.astype(BF16)
        for tap in range(9):
            a, b = tap // 3, tap % 3
            w = x_ref[b, :, pl.ds(ch * rc + a, rc)].reshape(mdev * cells, chans)
            p = jnp.dot(slt, w, preferred_element_type=F32)
            for dh in range(2):
                piece = tap * 2 + dh
                xh, off = piece // 9, (piece % 9) * 128
                for h in range(2):
                    acc[h, xh, off : off + 128] += p[
                        dh * 128 : dh * 128 + 128, h * 128 : h * 128 + 128
                    ]

    to_x(0).wait_recv()
    relay(0).start()

    @pl.loop(0, chunks)
    def _(ch):
        @pl.when(ch + 1 < chunks)
        def _():
            to_x(ch + 1).wait_recv()
            relay(ch + 1).start()

        to_core(ch).wait_recv()
        relay(ch).wait_recv()
        process(ch)

    edges = [
        rcopy(eo.at[1], ei.at[0], s_e.at[0], r_e.at[0], right),
        rcopy(eo.at[0], ei.at[1], s_e.at[1], r_e.at[1], left),
    ]
    for c in edges:
        c.start()
    st_core = rcopy(acc.at[1 - core], r1, s_st.at[0], r_st.at[0], cpeer)
    st_core.start()
    total = loss_ref[...]
    total = total[0:8, 0:128] + total[8:16, 0:128] + total[0:8, 128:256] + total[8:16, 128:256]
    l1[...] = total
    ls_core = rcopy(l1, lr1, s_ls.at[0], r_ls.at[0], cpeer)
    ls_core.start()

    for c in edges:
        c.wait_recv()
    col = lax.broadcasted_iota(jnp.int32, (cols, chans), 0)

    @pl.loop(0, mdev * rows)
    def _(i):
        m, row = i // rows, lax.rem(i, rows)
        v = sp[1, m, 1 + row].astype(F32)
        lo = jnp.where(col == 0, ei[0, pl.ds(i, 1)], pltpu.roll(v, 1, 0))
        hi = jnp.where(col == cols - 1, ei[1, pl.ds(i, 1)], pltpu.roll(v, cols - 1, 0))
        sp[0, m, 1 + row] = lo.astype(BF16)
        sp[2, m, 1 + row] = hi.astype(BF16)

    def grad_in(start, stop):
        @pl.loop(start, stop)
        def _(ch):
            total = None
            for a in range(3):
                for b in range(3):
                    w = sp[2 - b, :, pl.ds(ch * rc + 2 - a, rc)].reshape(mdev * cells, chans)
                    term = lax.dot_general(
                        w, k_ref[a * 3 + b], NT, preferred_element_type=F32
                    )
                    total = term if total is None else total + term
            gi_ref[:, pl.ds(ch * rc, rc)] = total.reshape(mdev, rc, cols, chans).astype(BF16)

    ls_core.wait_recv()
    l2[...] = l1[...] + lr1[...]
    ls_x = rcopy(l2, lr2, s_ls.at[1], r_ls.at[1], xpeer)
    ls_x.start()
    st_core.wait_recv()
    b2[...] = (acc[core, 1 - xx] + r1[1 - xx]).astype(BF16)
    st_x = rcopy(b2, r2, s_st.at[1], r_st.at[1], xpeer)
    st_x.start()
    grad_in(0, chunks // 2)

    ls_x.wait_recv()
    l3[...] = l2[...] + lr2[...]
    st_x.wait_recv()
    total = acc[core, xx] + r1[xx] + r2[...].astype(F32)
    r1[xx] = total
    b3[...] = total.astype(BF16)

    def part_of(i):
        return pl.ds(pl.multiple_of(i * part, 16), part)

    def to_strip(d, i):
        peer = lax.rem(s + d, n)
        return rcopy(
            b3.at[part_of(peer)], r3.at[i], s_sp.at[d], r_sp.at[i], {"space": peer}
        ), rcopy(l3, lr3.at[i], s_lp.at[d], r_lp.at[i], {"space": peer})

    @pl.loop(1, n)
    def _(d):
        for c in to_strip(d, s):
            c.start()

    grad_in(chunks // 2, chunks - chunks // 4)

    r2_total = r1[xx, part_of(s)]
    l_total = l3[...]

    def take(d, carry):
        g, l = carry
        peer = lax.rem(s + d, n)
        for c in to_strip(d, peer):
            c.wait_recv()
        return g + r3[peer].astype(F32), l + lr3[peer]

    r2_total, l_total = lax.fori_loop(1, n, take, (r2_total, l_total))
    gk_ref[core, xx, part_of(s)] = r2_total.astype(BF16)

    def gather(d, i):
        return rcopy(
            gk_ref.at[core, xx, part_of(i)], gk_ref.at[core, xx, part_of(i)],
            s_ag.at[d], r_ag.at[i], {"space": lax.rem(s + d, n)},
        )

    @pl.loop(1, n)
    def _(d):
        gather(d, s).start()

    grad_in(chunks - chunks // 4, chunks)
    loss_ref[0:8, 0:128] = l_total

    @pl.loop(1, n)
    def _(d):
        gather(d, lax.rem(s + d, n)).wait_recv()

    ag_x = rcopy(gk_ref.at[core, xx], gk_ref.at[core, xx], s_st.at[2], r_st.at[2], xpeer)
    ag_x.start()
    rcopy(gk_ref.at[core, 1 - xx], gk_ref.at[core, 1 - xx], s_st.at[2], r_st.at[2], xpeer).wait_recv()
    ag_c = rcopy(gk_ref.at[core], gk_ref.at[core], s_st.at[3], r_st.at[3], cpeer)
    ag_c.start()
    rcopy(gk_ref.at[1 - core], gk_ref.at[1 - core], s_st.at[3], r_st.at[3], cpeer).wait_recv()

    @pl.loop(0, chunks)
    def _(ch):
        to_x(ch).wait_send()
        to_core(ch).wait_send()
        relay(ch).wait_send()

    @pl.loop(1, n)
    def _(d):
        for c in to_strip(d, s):
            c.wait_send()
        gather(d, s).wait_send()

    for c in edges + [st_core, ls_core, ls_x, st_x, ag_x, ag_c]:
        c.wait_send()


def local(n, latents, targets, kernel):
    mdev, rows, cols, chans = latents.shape
    members = mdev * 4
    chunks = rows // ROW_CHUNK
    cells = ROW_CHUNK * cols
    x = rim(latents, n)
    part = -(-9 * 128 // (16 * n)) * 16
    hp = part * n
    vmem, dma = pltpu.VMEM, pltpu.SemaphoreType.DMA
    wire = vmem((chunks, mdev, cells, chans), WIRE)
    tile = vmem((8, 128), F32)
    gi, gk, loss = pl.pallas_call(
        functools.partial(body, n, members),
        name="crps_step",
        out_shape=(
            jax.ShapeDtypeStruct(latents.shape, BF16),
            jax.ShapeDtypeStruct((2, 2, hp, 128), BF16),
            jax.ShapeDtypeStruct((16, chans), F32),
        ),
        in_specs=[pl.BlockSpec(memory_space=vmem)] * 3,
        out_specs=(pl.BlockSpec(memory_space=vmem),) * 3,
        scratch_shapes=[
            vmem((chunks, mdev, cells, chans), F32),
            wire, wire, wire, wire,
            vmem((3, mdev, rows + 2, cols, chans), BF16),
            vmem((2, 2, hp, 128), F32),
            vmem((2, mdev * rows, chans), F32),
            vmem((2, mdev * rows, chans), F32),
            vmem((2, hp, 128), F32),
            vmem((hp, 128), BF16),
            vmem((hp, 128), BF16),
            vmem((hp, 128), BF16),
            vmem((n, part, 128), BF16),
            tile, tile, tile, tile, tile,
            vmem((n, 8, 128), F32),
            dma((chunks,)), dma((chunks,)), dma((chunks,)), dma((chunks,)),
            dma((chunks,)), dma((chunks,)),
            dma((2,)), dma((2,)), dma((4,)), dma((4,)), dma((2,)), dma((2,)),
            dma((n,)), dma((n,)), dma((n,)), dma((n,)), dma((n,)), dma((n,)),
        ],
        compiler_params=pltpu.CompilerParams(
            collective_id=0, has_side_effects=True, vmem_limit_bytes=48 * 2**20
        ),
    )(x, targets, kernel.reshape(9, chans, chans))
    longitude = cols * n
    gk = gk[:, :, : 9 * 128].reshape(2, 9, chans, 128).transpose(1, 0, 3, 2)
    grad_kernel = gk.astype(F32).reshape(3, 3, chans, chans) / (members * rows * longitude)
    loss = jnp.sum(loss[0:8, 0:128]) / (rows * longitude * chans)
    return loss, gi, grad_kernel


def solution(mesh):
    in_specs = (P("ens", None, "space", None), P(None, "space", None), P())
    out_specs = (P(), P("ens", None, "space", None), P())
    return jax.shard_map(
        functools.partial(local, mesh.shape["space"]),
        mesh=mesh, in_specs=in_specs, out_specs=out_specs, check_vma=False,
    )
```

time: 302 us -> 88.7 us (0.29)
  the two profiles are of different devices: /device:TPU:1 before, /device:TPU:25 now
where the time goes in v1:
time: 88.7 us; the launch traced here: 88.4 us
  Pallas kernels  72.8 us (82%)
  local copies, waits for them, and re-layouts  6.75 us (8%)
  other arithmetic  3.37 us (4%)
  between operations  2.48 us (3%)
  starting transfers between devices  2.42 us (3%)
    pallas_call x1, Pallas kernels, local(): pl.pallas_call(functools.partial(body, n, members), name='crps_step', out...  72.8 us
    another operation x3, other arithmetic, rim(): jnp.stack([left, block, right])  2.62 us
    slice x1, local copies, waits for them, and re-layouts, rim(): left = jnp.concatenate([low, block[:, :, :cols - 1]], axis=2)  2.35 us
    div x1, local copies, waits for them, and re-layouts, local(): gk.astype(F32).reshape(3, 3, chans, chans) / (members * rows * longitude)  1.95 us
  transfers between devices with their start and end apart: 2, of which 1 were waited for; matrix products, arithmetic and copies ran while one was open for 3% of the time, Pallas kernels for 0%

profile of v1, /device:TPU:25, one launch (start us, length us, event | category | flops | bytes accessed | tf_op | source)
XLA Modules:
  0.0 88.4 jit_solution(10319742340984567401)
XLA Ops:
  0.6 1.1 %fusion.6 = (bf16[2,32,1,256]{3,2,1,0:T(2,128)(2,1)S(1)}, bf16[2,32,1,256]{3,2,1,0:T(2,128)(2,1)S(1)}) fusion(bf16[2,32,32,256]{3,2,1,0:T(8,128)(2,1)} %param.3), kind=kLoop, calls=%fused_computation.12 | loop fusion | bytes 131072 | tf_op jit(solution)/shard_map/slice | solution.py:21
  1.8 1.3 %collective-permute-start = (bf16[2,32,1,256]{3,2,1,0:T(2,128)(2,1)S(1)}, bf16[2,32,1,256]{3,2,1,0:T(2,128)(2,1)S(1)}, u32[]{:S(2)}, u32[]{:S(2)}) collective-permute-start(bf16[2,32,1,256]{3,2,1,0:T(2,128)(2,1)S(1)} %get-tuple-element.9), channel_id=1, source_target_pairs={{0,1},{1,2},{2,3},{3,4},{4,5},{5,6},{6,7},{7,0},{8,9},{9,10},{10,1... | collective-permute-start | bytes 98312 | tf_op jit(solution)/shard_map/ppermute | solution.py:21
  3.1 0.0 copy-start.2
  3.1 1.1 %collective-permute-start.1 = (bf16[2,32,1,256]{3,2,1,0:T(2,128)(2,1)S(1)}, bf16[2,32,1,256]{3,2,1,0:T(2,128)(2,1)S(1)}, u32[]{:S(2)}, u32[]{:S(2)}) collective-permute-start(bf16[2,32,1,256]{3,2,1,0:T(2,128)(2,1)S(1)} %get-tuple-element.10), channel_id=1, source_target_pairs={{1,0},{2,1},{3,2},{4,3},{5,4},{6,5},{7,6},{0,7},{9,8},{10,9},{11,1... | collective-permute-start | bytes 98312 | tf_op jit(solution)/shard_map/ppermute | solution.py:22
  4.2 2.3 %fusion.7 = (bf16[2,32,31,256]{3,2,1,0:T(8,128)(2,1)S(1)}, bf16[2,32,31,256]{3,2,1,0:T(8,128)(2,1)S(1)}) fusion(bf16[2,32,32,256]{3,2,1,0:T(8,128)(2,1)} %param.3), kind=kLoop, calls=%fused_computation.13 | loop fusion | bytes 4063232 | tf_op jit(solution)/shard_map/slice | solution.py:23
  6.5 0.0 collective-permute-done
  6.6 0.6 maximum_bitcast_fusion
  7.1 0.6 collective-permute-done.1
  7.7 0.2 maximum_bitcast_fusion.1
  7.9 0.0 copy-start
  7.9 0.0 copy-start.1
  8.0 0.0 copy-done.2
  8.0 1.8 %fusion.5.x_ref = bf16[3,2,34,32,256]{4,3,2,1,0:T(8,128)(2,1)} fusion(bf16[1,2,32,32,256]{4,3,2,1,0:T(8,128)(2,1)S(1)} %maximum_bitcast_fusion.1, bf16[1,2,32,32,256]{4,3,2,1,0:T(8,128)(2,1)S(1)} %bitcast.11, bf16[1,2,32,32,256]{4,3,2,1,0:T(8,128)(2,1)S(1)} %maximum_bitcast_fusion), kind=kLoop, calls=%fused_computation.7 | loop fusion | flops 20054016 | bytes 6488064 | tf_op jit(solution)/shard_map/stack | solution.py:25
  9.8 0.0 copy-done
  9.8 0.3 copy-done.1
  10.1 72.8 %crps_step.1 = (bf16[2,32,32,256]{3,2,1,0:T(8,128)(2,1)S(1)}, bf16[2,2,1152,128]{3,2,1,0:T(8,128)(2,1)S(1)}, f32[16,256]{1,0:T(8,128)S(1)}) custom-call(bf16[3,2,34,32,256]{4,3,2,1,0:T(8,128)(2,1)} %fusion.5.x_ref, bf16[32,32,256]{2,1,0:T(8,128)(2,1)S(1)} %copy-done.1, bf16[9,256,256]{2,1,0:T(8,128)(2,1)S(1)} %bitcast.10), custom_call_target="tpu_custom_call" | custom-call | tf_op jit(solution)/shard_map/crps_step/pallas_call | solution.py:303
  83.0 0.6 slice_reduce_fusion
  83.6 0.2 convert_multiply_fusion
  83.7 2.0 %copy.6 = f32[9,2,128,256]{3,2,1,0:T(8,128)} copy(f32[9,2,128,256]{2,3,0,1:T(8,128)S(1)} %bitcast.12) | data formatting | bytes 4718592 | tf_op jit(solution)/shard_map/div | solution.py:338
  86.3 1.0 %copy.8 = bf16[2,32,32,256]{3,2,1,0:T(8,128)(2,1)} copy(bf16[2,32,32,256]{3,2,1,0:T(8,128)(2,1)S(1)} %get-tuple-element.17) | data formatting | bytes 2097152
Async XLA Ops:
  1.8 4.8 %collective-permute-start = (bf16[2,32,1,256]{3,2,1,0:T(2,128)(2,1)S(1)}, bf16[2,32,1,256]{3,2,1,0:T(2,128)(2,1)S(1)}, u32[]{:S(2)}, u32[]{:S(2)}) collective-permute-start(bf16[2,32,1,256]{3,2,1,0:T(2,128)(2,1)S(1)} %get-tuple-element.9), channel_id=1, source_target_pairs={{0,1},{1,2},{2,3},{3,4},{4,5},{5,6},{6,7},{7,0},{8,9},{9,10},{10,1... | collective-permute-start | bytes 98312 | tf_op jit(solution)/shard_map/ppermute | solution.py:21
  3.1 4.9 %copy-start.2 = (bf16[2,32,32,256]{3,2,1,0:T(8,128)(2,1)S(1)}, bf16[2,32,32,256]{3,2,1,0:T(8,128)(2,1)}, u32[]{:S(2)}) copy-start(bf16[2,32,32,256]{3,2,1,0:T(8,128)(2,1)} %param.3) | copy-start | bytes 3145732
  3.1 4.6 %collective-permute-start.1 = (bf16[2,32,1,256]{3,2,1,0:T(2,128)(2,1)S(1)}, bf16[2,32,1,256]{3,2,1,0:T(2,128)(2,1)S(1)}, u32[]{:S(2)}, u32[]{:S(2)}) collective-permute-start(bf16[2,32,1,256]{3,2,1,0:T(2,128)(2,1)S(1)} %get-tuple-element.10), channel_id=1, source_target_pairs={{1,0},{2,1},{3,2},{4,3},{5,4},{6,5},{7,6},{0,7},{9,8},{10,9},{11,1... | collective-permute-start | bytes 98312 | tf_op jit(solution)/shard_map/ppermute | solution.py:22
  7.9 1.9 %copy-start = (bf16[3,3,256,256]{3,2,1,0:T(8,128)(2,1)S(1)}, bf16[3,3,256,256]{3,2,1,0:T(8,128)(2,1)}, u32[]{:S(2)}) copy-start(bf16[3,3,256,256]{3,2,1,0:T(8,128)(2,1)} %param.5) | copy-start | bytes 3538948
  7.9 2.2 %copy-start.1 = (bf16[32,32,256]{2,1,0:T(8,128)(2,1)S(1)}, bf16[32,32,256]{2,1,0:T(8,128)(2,1)}, u32[]{:S(2)}) copy-start(bf16[32,32,256]{2,1,0:T(8,128)(2,1)} %t_ref.1) | copy-start | bytes 1572868

commit v2 on v1

--- a/solution.py
+++ b/solution.py
@@ -10,34 +10,25 @@
 smoothing = 0.1
 WIRE = jnp.bfloat16
 ROW_CHUNK = 4
+PIECES = 3
 F32, BF16 = jnp.float32, jnp.bfloat16
 NT = (((1,), (1,)), ((), ()))
 
 
-def rim(block, count):
-    cols = block.shape[2]
-    forward = [(i, (i + 1) % count) for i in range(count)]
-    backward = [(t, s) for s, t in forward]
-    low = lax.ppermute(block[:, :, cols - 1 :], "space", forward)
-    high = lax.ppermute(block[:, :, :1], "space", backward)
-    left = jnp.concatenate([low, block[:, :, : cols - 1]], axis=2)
-    right = jnp.concatenate([block[:, :, 1:], high], axis=2)
-    return jnp.pad(jnp.stack([left, block, right]), ((0, 0), (0, 0), (1, 1), (0, 0), (0, 0)))
-
-
 def body(
     n, members,
-    x_ref, t_ref, k_ref,
+    lat_ref, t_ref, k_ref,
     gi_ref, gk_ref, loss_ref,
-    f_own, own, co, xp, xc, sp, acc, eo, ei, r1, b2, r2, b3, r3, l1, lr1, l2, lr2, l3, lr3,
-    s_x, r_x, s_c, r_c, s_l, r_l, s_e, r_e, s_st, r_st, s_ls, r_ls, s_sp, r_sp, s_lp, r_lp,
-    s_ag, r_ag,
+    x_ref, leo, lei, f_own, own, co, xp, xc, sp, acc, eo, ei, r1, b2, r2, b3, r3, l1, lr1, l2, lr2, l3, lr3,
+    s_x, r_x, s_c, r_c, s_l, r_l, s_e, r_e, s_st, r_st, s_x2, r_x2, s_ls, r_ls, s_sp, r_sp, s_lp, r_lp,
+    s_ag, r_ag, s_le, r_le, s_ax, r_ax, s_ac, r_ac,
 ):
     mdev, rows, cols, chans = gi_ref.shape
     rc = ROW_CHUNK
     chunks = rows // rc
     cells = rc * cols
-    part = b3.shape[0] // n
+    part = b3.shape[0] // (n * PIECES)
+    span = part * n
     e = lax.axis_index("ens")
     s = lax.axis_index("space")
     core = lax.rem(e, 2)
@@ -64,7 +55,45 @@
             device_id_type=pl.DeviceIdType.MESH,
         )
 
+    @pl.loop(0, mdev * rows)
+    def _(i):
+        m, row = i // rows, lax.rem(i, rows)
+        v = lat_ref[m, row]
+        x_ref[1, m, 1 + row] = v
+        v = v.astype(F32)
+        leo[0, pl.ds(i, 1)] = v[0:1]
+        leo[1, pl.ds(i, 1)] = v[cols - 1 : cols]
+
     pl.semaphore_wait(barrier, n + 1)
+    lat_edges = [
+        rcopy(leo.at[1], lei.at[0], s_le.at[0], r_le.at[0], right),
+        rcopy(leo.at[0], lei.at[1], s_le.at[1], r_le.at[1], left),
+    ]
+    for c in lat_edges:
+        c.start()
+    acc[...] = jnp.zeros_like(acc)
+    loss_ref[...] = jnp.zeros_like(loss_ref)
+    for c in range(3):
+        for r in (0, rows + 1):
+            sp[c, :, r] = jnp.zeros((mdev, cols, chans), BF16)
+            x_ref[c, :, r] = jnp.zeros((mdev, cols, chans), BF16)
+    for c in lat_edges:
+        c.wait_recv()
+
+    col = lax.broadcasted_iota(jnp.int32, (cols, chans), 0)
+
+    def shift(ref, edge, m, row):
+        i = m * rows + row
+        v = ref[1, m, 1 + row].astype(F32)
+        lo = jnp.where(col == 0, edge[0, pl.ds(i, 1)], pltpu.roll(v, 1, 0))
+        hi = jnp.where(col == cols - 1, edge[1, pl.ds(i, 1)], pltpu.roll(v, cols - 1, 0))
+        ref[0, m, 1 + row] = lo.astype(BF16)
+        ref[2, m, 1 + row] = hi.astype(BF16)
+
+    @pl.loop(0, mdev * rows)
+    def _(i):
+        shift(x_ref, lei, i // rows, lax.rem(i, rows))
+
 
     def to_x(ch):
         return rcopy(own.at[ch], xp.at[ch], s_x.at[ch], r_x.at[ch], xpeer)
@@ -88,12 +117,6 @@
         own[ch] = total.astype(WIRE)
         to_x(ch).start()
         to_core(ch).start()
-
-    acc[...] = jnp.zeros_like(acc)
-    loss_ref[...] = jnp.zeros_like(loss_ref)
-    for c in range(3):
-        for r in (0, rows + 1):
-            sp[c, :, r] = jnp.zeros((mdev, cols, chans), BF16)
 
     def smooth(gap):
         square = gap * gap + smoothing * smoothing
@@ -169,26 +192,47 @@
     ]
     for c in edges:
         c.start()
-    st_core = rcopy(acc.at[1 - core], r1, s_st.at[0], r_st.at[0], cpeer)
-    st_core.start()
+
+    def span_of(p):
+        return pl.ds(p * span, span)
+
+    def part_of(p, i):
+        return pl.ds(pl.multiple_of(p * span + i * part, 16), part)
+
+    st_core = {}
+    for p in range(PIECES):
+        for j in range(2):
+            h = 1 - xx if j == 0 else xx
+            st_core[p, j] = rcopy(
+                acc.at[1 - core, h, span_of(p)], r1.at[h, span_of(p)],
+                s_st.at[p, j], r_st.at[p, j], cpeer,
+            )
+            st_core[p, j].start()
     total = loss_ref[...]
     total = total[0:8, 0:128] + total[8:16, 0:128] + total[0:8, 128:256] + total[8:16, 128:256]
     l1[...] = total
     ls_core = rcopy(l1, lr1, s_ls.at[0], r_ls.at[0], cpeer)
     ls_core.start()
 
+    st_x = []
+    for p in range(PIECES):
+        st_core[p, 0].wait_recv()
+        b2[span_of(p)] = (
+            acc[core, 1 - xx, span_of(p)] + r1[1 - xx, span_of(p)]
+        ).astype(BF16)
+        st_x.append(rcopy(b2.at[span_of(p)], r2.at[span_of(p)], s_x2.at[p], r_x2.at[p], xpeer))
+        st_x[p].start()
+    ls_core.wait_recv()
+    l2[...] = l1[...] + lr1[...]
+    ls_x = rcopy(l2, lr2, s_ls.at[1], r_ls.at[1], xpeer)
+    ls_x.start()
+
     for c in edges:
         c.wait_recv()
-    col = lax.broadcasted_iota(jnp.int32, (cols, chans), 0)
 
     @pl.loop(0, mdev * rows)
     def _(i):
-        m, row = i // rows, lax.rem(i, rows)
-        v = sp[1, m, 1 + row].astype(F32)
-        lo = jnp.where(col == 0, ei[0, pl.ds(i, 1)], pltpu.roll(v, 1, 0))
-        hi = jnp.where(col == cols - 1, ei[1, pl.ds(i, 1)], pltpu.roll(v, cols - 1, 0))
-        sp[0, m, 1 + row] = lo.astype(BF16)
-        sp[2, m, 1 + row] = hi.astype(BF16)
+        shift(sp, ei, i // rows, lax.rem(i, rows))
 
     def grad_in(start, stop):
         @pl.loop(start, stop)
@@ -203,75 +247,89 @@
                     total = term if total is None else total + term
             gi_ref[:, pl.ds(ch * rc, rc)] = total.reshape(mdev, rc, cols, chans).astype(BF16)
 
-    ls_core.wait_recv()
-    l2[...] = l1[...] + lr1[...]
-    ls_x = rcopy(l2, lr2, s_ls.at[1], r_ls.at[1], xpeer)
-    ls_x.start()
-    st_core.wait_recv()
-    b2[...] = (acc[core, 1 - xx] + r1[1 - xx]).astype(BF16)
-    st_x = rcopy(b2, r2, s_st.at[1], r_st.at[1], xpeer)
-    st_x.start()
-    grad_in(0, chunks // 2)
+    def to_strip(p, d, i):
+        peer = lax.rem(s + d, n)
+        return rcopy(
+            b3.at[part_of(p, peer)], r3.at[p, i], s_sp.at[p, d], r_sp.at[p, i], {"space": peer}
+        )
+
+    def loss_to_strip(d, i):
+        return rcopy(l3, lr3.at[i], s_lp.at[d], r_lp.at[i], {"space": lax.rem(s + d, n)})
+
+    def gather(p, d, i):
+        return rcopy(
+            gk_ref.at[core, xx, part_of(p, i)], gk_ref.at[core, xx, part_of(p, i)],
+            s_ag.at[p, d], r_ag.at[p, i], {"space": lax.rem(s + d, n)},
+        )
+
+    marks = [chunks * i // 8 for i in range(9)]
+    for p in range(PIECES):
+        grad_in(marks[p], marks[p + 1])
+        st_core[p, 1].wait_recv()
+        st_x[p].wait_recv()
+        total = acc[core, xx, span_of(p)] + r1[xx, span_of(p)] + r2[span_of(p)].astype(F32)
+        r1[xx, span_of(p)] = total
+        b3[span_of(p)] = total.astype(BF16)
+
+        @pl.loop(1, n)
+        def _(d):
+            to_strip(p, d, s).start()
 
     ls_x.wait_recv()
     l3[...] = l2[...] + lr2[...]
-    st_x.wait_recv()
-    total = acc[core, xx] + r1[xx] + r2[...].astype(F32)
-    r1[xx] = total
-    b3[...] = total.astype(BF16)
-
-    def part_of(i):
-        return pl.ds(pl.multiple_of(i * part, 16), part)
-
-    def to_strip(d, i):
-        peer = lax.rem(s + d, n)
-        return rcopy(
-            b3.at[part_of(peer)], r3.at[i], s_sp.at[d], r_sp.at[i], {"space": peer}
-        ), rcopy(l3, lr3.at[i], s_lp.at[d], r_lp.at[i], {"space": peer})
 
     @pl.loop(1, n)
     def _(d):
-        for c in to_strip(d, s):
-            c.start()
-
-    grad_in(chunks // 2, chunks - chunks // 4)
-
-    r2_total = r1[xx, part_of(s)]
-    l_total = l3[...]
-
-    def take(d, carry):
-        g, l = carry
+        loss_to_strip(d, s).start()
+
+    for p in range(PIECES):
+        grad_in(marks[PIECES + p], marks[PIECES + p + 1])
+
+        def take(d, g):
+            peer = lax.rem(s + d, n)
+            to_strip(p, d, peer).wait_recv()
+            return g + r3[p, peer].astype(F32)
+
+        total = lax.fori_loop(1, n, take, r1[xx, part_of(p, s)])
+        gk_ref[core, xx, part_of(p, s)] = total.astype(BF16)
+
+        @pl.loop(1, n)
+        def _(d):
+            gather(p, d, s).start()
+
+    grad_in(marks[2 * PIECES], chunks)
+
+    def take_loss(d, l):
         peer = lax.rem(s + d, n)
-        for c in to_strip(d, peer):
-            c.wait_recv()
-        return g + r3[peer].astype(F32), l + lr3[peer]
-
-    r2_total, l_total = lax.fori_loop(1, n, take, (r2_total, l_total))
-    gk_ref[core, xx, part_of(s)] = r2_total.astype(BF16)
-
-    def gather(d, i):
-        return rcopy(
-            gk_ref.at[core, xx, part_of(i)], gk_ref.at[core, xx, part_of(i)],
-            s_ag.at[d], r_ag.at[i], {"space": lax.rem(s + d, n)},
-        )
-
-    @pl.loop(1, n)
-    def _(d):
-        gather(d, s).start()
-
-    grad_in(chunks - chunks // 4, chunks)
-    loss_ref[0:8, 0:128] = l_total
-
-    @pl.loop(1, n)
-    def _(d):
-        gather(d, lax.rem(s + d, n)).wait_recv()
-
-    ag_x = rcopy(gk_ref.at[core, xx], gk_ref.at[core, xx], s_st.at[2], r_st.at[2], xpeer)
-    ag_x.start()
-    rcopy(gk_ref.at[core, 1 - xx], gk_ref.at[core, 1 - xx], s_st.at[2], r_st.at[2], xpeer).wait_recv()
-    ag_c = rcopy(gk_ref.at[core], gk_ref.at[core], s_st.at[3], r_st.at[3], cpeer)
-    ag_c.start()
-    rcopy(gk_ref.at[1 - core], gk_ref.at[1 - core], s_st.at[3], r_st.at[3], cpeer).wait_recv()
+        loss_to_strip(d, peer).wait_recv()
+        return l + lr3[peer]
+
+    loss_ref[0:8, 0:128] = lax.fori_loop(1, n, take_loss, l3[...])
+
+    ag_x, ag_c = [], []
+    for p in range(PIECES):
+
+        @pl.loop(1, n)
+        def _(d):
+            gather(p, d, lax.rem(s + d, n)).wait_recv()
+
+        mine = gk_ref.at[core, xx, span_of(p)]
+        ag_x.append(rcopy(mine, mine, s_ax.at[p], r_ax.at[p], xpeer))
+        ag_x[p].start()
+        ag_c.append(rcopy(mine, mine, s_ac.at[p, 0], r_ac.at[p, 0], cpeer))
+        ag_c[-1].start()
+
+    for p in range(PIECES):
+        theirs = gk_ref.at[core, 1 - xx, span_of(p)]
+        rcopy(theirs, theirs, s_ax.at[p], r_ax.at[p], xpeer).wait_recv()
+        ag_c.append(rcopy(theirs, theirs, s_ac.at[p, 1], r_ac.at[p, 1], cpeer))
+        ag_c[-1].start()
+
+    for p in range(PIECES):
+        for j in range(2):
+            h = xx if j == 0 else 1 - xx
+            theirs = gk_ref.at[1 - core, h, span_of(p)]
+            rcopy(theirs, theirs, s_ac.at[p, j], r_ac.at[p, j], cpeer).wait_recv()
 
     @pl.loop(0, chunks)
     def _(ch):
@@ -281,11 +339,12 @@
 
     @pl.loop(1, n)
     def _(d):
-        for c in to_strip(d, s):
-            c.wait_send()
-        gather(d, s).wait_send()
-
-    for c in edges + [st_core, ls_core, ls_x, st_x, ag_x, ag_c]:
+        for p in range(PIECES):
+            to_strip(p, d, s).wait_send()
+            gather(p, d, s).wait_send()
+        loss_to_strip(d, s).wait_send()
+
+    for c in lat_edges + edges + list(st_core.values()) + st_x + [ls_core, ls_x] + ag_x + ag_c:
         c.wait_send()
 
 
@@ -294,9 +353,8 @@
     members = mdev * 4
     chunks = rows // ROW_CHUNK
     cells = ROW_CHUNK * cols
-    x = rim(latents, n)
-    part = -(-9 * 128 // (16 * n)) * 16
-    hp = part * n
+    part = -(-9 * 128 // (16 * n * PIECES)) * 16
+    hp = part * n * PIECES
     vmem, dma = pltpu.VMEM, pltpu.SemaphoreType.DMA
     wire = vmem((chunks, mdev, cells, chans), WIRE)
     tile = vmem((8, 128), F32)
@@ -311,6 +369,9 @@
         in_specs=[pl.BlockSpec(memory_space=vmem)] * 3,
         out_specs=(pl.BlockSpec(memory_space=vmem),) * 3,
         scratch_shapes=[
+            vmem((3, mdev, rows + 2, cols, chans), BF16),
+            vmem((2, mdev * rows, chans), F32),
+            vmem((2, mdev * rows, chans), F32),
             vmem((chunks, mdev, cells, chans), F32),
             wire, wire, wire, wire,
             vmem((3, mdev, rows + 2, cols, chans), BF16),
@@ -321,18 +382,20 @@
             vmem((hp, 128), BF16),
             vmem((hp, 128), BF16),
             vmem((hp, 128), BF16),
-            vmem((n, part, 128), BF16),
+            vmem((PIECES, n, part, 128), BF16),
             tile, tile, tile, tile, tile,
             vmem((n, 8, 128), F32),
             dma((chunks,)), dma((chunks,)), dma((chunks,)), dma((chunks,)),
             dma((chunks,)), dma((chunks,)),
-            dma((2,)), dma((2,)), dma((4,)), dma((4,)), dma((2,)), dma((2,)),
-            dma((n,)), dma((n,)), dma((n,)), dma((n,)), dma((n,)), dma((n,)),
+            dma((2,)), dma((2,)), dma((PIECES, 2)), dma((PIECES, 2)), dma((PIECES,)), dma((PIECES,)),
+            dma((2,)), dma((2,)), dma((PIECES, n)), dma((PIECES, n)), dma((n,)), dma((n,)),
+            dma((PIECES, n)), dma((PIECES, n)), dma((2,)), dma((2,)),
+            dma((PIECES,)), dma((PIECES,)), dma((PIECES, 2)), dma((PIECES, 2)),
         ],
         compiler_params=pltpu.CompilerParams(
             collective_id=0, has_side_effects=True, vmem_limit_bytes=48 * 2**20
         ),
-    )(x, targets, kernel.reshape(9, chans, chans))
+    )(latents, targets, kernel.reshape(9, chans, chans))
     longitude = cols * n
     gk = gk[:, :, : 9 * 128].reshape(2, 9, chans, 128).transpose(1, 0, 3, 2)
     grad_kernel = gk.astype(F32).reshape(3, 3, chans, chans) / (members * rows * longitude)

time: 88.7 us -> 79.6 us (0.90)
  the two profiles are of different devices: /device:TPU:25 before, /device:TPU:1 now
where the time goes in v2:
time: 79.6 us; the launch traced here: 79.3 us
  Pallas kernels  67.2 us (84%)
  local copies, waits for them, and re-layouts  7.54 us (9%)
  between operations  2.43 us (3%)
  other arithmetic  2.17 us (3%)
    pallas_call x1, Pallas kernels, local(): pl.pallas_call(functools.partial(body, n, members), name='crps_step', out...  67.2 us
    unnamed x7, local copies, waits for them, and re-layouts  4.5 us
    div x1, local copies, waits for them, and re-layouts, local(): gk.astype(F32).reshape(3, 3, chans, chans) / (members * rows * longitude)  3.04 us

profile of v2, /device:TPU:1, one launch (start us, length us, event | category | flops | bytes accessed | tf_op | source)
XLA Modules:
  0.0 79.3 jit_solution(6856068651518930532)
XLA Ops:
  0.6 0.0 copy-start
  0.6 1.3 %copy-done = bf16[3,3,256,256]{3,2,1,0:T(8,128)(2,1)S(1)} copy-done((bf16[3,3,256,256]{3,2,1,0:T(8,128)(2,1)S(1)}, bf16[3,3,256,256]{3,2,1,0:T(8,128)(2,1)}, u32[]{:S(2)}) %copy-start) | copy-done | bytes 1179672
  1.9 0.0 copy-start.1
  1.9 1.2 %copy-done.1 = bf16[2,32,32,256]{3,2,1,0:T(8,128)(2,1)S(1)} copy-done((bf16[2,32,32,256]{3,2,1,0:T(8,128)(2,1)S(1)}, bf16[2,32,32,256]{3,2,1,0:T(8,128)(2,1)}, u32[]{:S(2)}) %copy-start.1) | copy-done | bytes 1048600
  3.1 0.0 copy-start.2
  3.1 1.0 %copy-done.2 = bf16[32,32,256]{2,1,0:T(8,128)(2,1)S(1)} copy-done((bf16[32,32,256]{2,1,0:T(8,128)(2,1)S(1)}, bf16[32,32,256]{2,1,0:T(8,128)(2,1)}, u32[]{:S(2)}) %copy-start.2) | copy-done | bytes 524312
  4.2 67.2 %crps_step.1 = (bf16[2,32,32,256]{3,2,1,0:T(8,128)(2,1)S(1)}, bf16[2,2,1152,128]{3,2,1,0:T(8,128)(2,1)S(1)}, f32[16,256]{1,0:T(8,128)S(1)}) custom-call(bf16[2,32,32,256]{3,2,1,0:T(8,128)(2,1)S(1)} %copy-done.1, bf16[32,32,256]{2,1,0:T(8,128)(2,1)S(1)} %copy-done.2, bf16[9,256,256]{2,1,0:T(8,128)(2,1)S(1)} %bitcast.5), custom_call_target="tpu_custom_call" | custom-call | tf_op jit(solution)/shard_map/crps_step/pallas_call | solution.py:361
  71.3 0.6 slice_reduce_fusion
  72.6 1.6 %convert_multiply_fusion = f32[2,2,1152,128]{3,2,1,0:T(8,128)} fusion(bf16[2,2,1152,128]{3,2,1,0:T(8,128)(2,1)S(1)} %get-tuple-element.8), kind=kLoop, calls=%fused_computation | loop fusion | flops 1179648 | bytes 3538944 | tf_op jit(solution)/shard_map/div | solution.py:401
  74.2 3.0 %copy.6 = f32[9,2,128,256]{3,2,1,0:T(8,128)} copy(f32[9,2,128,256]{2,3,0,1:T(8,128)} %bitcast.6) | data formatting | bytes 4718592 | tf_op jit(solution)/shard_map/div | solution.py:401
  77.2 1.0 %copy.8 = bf16[2,32,32,256]{3,2,1,0:T(8,128)(2,1)} copy(bf16[2,32,32,256]{3,2,1,0:T(8,128)(2,1)S(1)} %get-tuple-element.13) | data formatting | bytes 2097152
Async XLA Ops:
  0.6 1.3 %copy-start = (bf16[3,3,256,256]{3,2,1,0:T(8,128)(2,1)S(1)}, bf16[3,3,256,256]{3,2,1,0:T(8,128)(2,1)}, u32[]{:S(2)}) copy-start(bf16[3,3,256,256]{3,2,1,0:T(8,128)(2,1)} %param.5) | copy-start | bytes 3538948
  1.9 1.2 %copy-start.1 = (bf16[2,32,32,256]{3,2,1,0:T(8,128)(2,1)S(1)}, bf16[2,32,32,256]{3,2,1,0:T(8,128)(2,1)}, u32[]{:S(2)}) copy-start(bf16[2,32,32,256]{3,2,1,0:T(8,128)(2,1)} %lat_ref.1) | copy-start | bytes 3145732
  3.1 1.0 %copy-start.2 = (bf16[32,32,256]{2,1,0:T(8,128)(2,1)S(1)}, bf16[32,32,256]{2,1,0:T(8,128)(2,1)}, u32[]{:S(2)}) copy-start(bf16[32,32,256]{2,1,0:T(8,128)(2,1)} %t_ref.1) | copy-start | bytes 1572868

commit v3 on v2

v3 whole, which is shorter than its diff:
```python
import functools

import jax
import jax.numpy as jnp
from jax import lax
from jax.experimental import pallas as pl
from jax.experimental.pallas import tpu as pltpu
from jax.sharding import PartitionSpec as P

smoothing = 0.1
PIECES = 3
F32, BF16 = jnp.float32, jnp.bfloat16
NT = (((1,), (1,)), ((), ()))


def body(
    n, members,
    lat_ref, t_ref, k_ref,
    gi_ref, gk_ref, loss_ref,
    x_ref, leo, lei, fld, sp, acc, eo, ei, gib, r1, b2, r2, b3, r3, l1, lr1, l2, lr2, l3, lr3,
    s_x, r_x, s_le, r_le, s_e, r_e, s_h, r_h, s_g, r_g,
    s_st, r_st, s_x2, r_x2, s_ls, r_ls, s_sp, r_sp, s_lp, r_lp,
    s_ag, r_ag, s_ax, r_ax, s_ac, r_ac,
):
    mdev, rows, cols, chans = gi_ref.shape
    own_rows = rows // 4
    slots = own_rows + 2
    cells = members * cols
    part = b3.shape[0] // (n * PIECES)
    span = part * n
    e = lax.axis_index("ens")
    s = lax.axis_index("space")
    core = lax.rem(e, 2)
    xx = e // 2
    cpeer = {"ens": xx * 2 + (1 - core)}
    xpeer = {"ens": (1 - xx) * 2 + core}
    right_s = lax.rem(s + 1, n)
    left_s = lax.rem(s + n - 1, n)
    right, left = {"space": right_s}, {"space": left_s}
    MESH = pl.DeviceIdType.MESH

    def rcopy(src, dst, ss, rs, dev):
        return pltpu.make_async_remote_copy(
            src_ref=src, dst_ref=dst, send_sem=ss, recv_sem=rs,
            device_id=dev, device_id_type=MESH,
        )

    def ens_at(d):
        return lax.rem(e + d, 4)

    blank = jnp.zeros((members, cols, chans), BF16)
    for c in range(3):
        for r in (0, slots - 1):
            sp[c, r] = blank
            x_ref[c, r] = blank
    for side in range(2):
        for r in (0, rows + 1):
            leo[side, r] = jnp.zeros((mdev, chans), F32)

    barrier = pltpu.get_barrier_semaphore()
    for d in range(1, 4):
        for strip in (s, right_s, left_s):
            pl.semaphore_signal(
                barrier, inc=1, device_id={"ens": ens_at(d), "space": strip}, device_id_type=MESH
            )

    @pl.loop(1, n)
    def _(d):
        pl.semaphore_signal(
            barrier, inc=1, device_id={"space": lax.rem(s + d, n)}, device_id_type=MESH
        )

    @pl.loop(0, rows)
    def _(row):
        for m in range(mdev):
            v = lat_ref[m, row].astype(F32)
            leo[0, 1 + row, m : m + 1] = v[0:1]
            leo[1, 1 + row, m : m + 1] = v[cols - 1 : cols]

    pl.semaphore_wait(barrier, n - 1 + 9)

    def edge_of(side, d, src):
        to = ens_at(d)
        return rcopy(
            leo.at[side, pl.ds(to * own_rows, slots)], lei.at[1 - side, src],
            s_le.at[side, d], r_le.at[1 - side, src],
            {"ens": to, "space": left_s if side == 0 else right_s},
        )

    for d in (2, 3, 1, 0):
        for side in range(2):
            edge_of(side, d, e).start()

    def row_of(d, to, slot, src):
        row = to * own_rows - 1 + slot
        inside = (row >= 0) & (row < rows)
        return inside, rcopy(
            lat_ref.at[:, jnp.clip(row, 0, rows - 1)], x_ref.at[1, slot, pl.ds(mdev * src, mdev)],
            s_x.at[d, slot], r_x.at[src, slot], {"ens": to},
        )

    @pl.loop(0, slots)
    def _(slot):
        for d in (2, 3, 1):
            inside, c = row_of(d, ens_at(d), slot, e)

            @pl.when(inside)
            def _():
                c.start()

        row = e * own_rows - 1 + slot

        @pl.when((row >= 0) & (row < rows))
        def _():
            for m in range(mdev):
                x_ref[1, slot, e * mdev + m] = lat_ref[m, row]

    acc[...] = jnp.zeros_like(acc)
    loss_ref[...] = jnp.zeros_like(loss_ref)
    for d in (0, 1, 2, 3):
        for side in range(2):
            edge_of(side, d, ens_at(d)).wait_recv()

    col = lax.broadcasted_iota(jnp.int32, (cols, chans), 0)

    def shift(ref, slot, edge):
        for mem in range(members):
            v = ref[1, slot, mem].astype(F32)
            lo = jnp.where(col == 0, edge(0, mem), pltpu.roll(v, 1, 0))
            hi = jnp.where(col == cols - 1, edge(1, mem), pltpu.roll(v, cols - 1, 0))
            ref[0, slot, mem] = lo.astype(BF16)
            ref[2, slot, mem] = hi.astype(BF16)

    def ready(slot):
        for d in range(1, 4):
            inside, c = row_of(d, e, slot, ens_at(d))

            @pl.when(inside)
            def _():
                c.wait_recv()

        shift(
            x_ref, slot,
            lambda side, mem: lei[side, mem // mdev, slot, mem % mdev : mem % mdev + 1],
        )

    def smooth(gap):
        square = gap * gap + smoothing * smoothing
        inv = lax.rsqrt(square)
        return gap * inv, square * inv

    for slot in range(2):
        ready(slot)

    @pl.loop(0, own_rows)
    def _(i):
        ready(i + 2)
        total = None
        for a in range(3):
            for b in range(3):
                w = x_ref[b, i + a].reshape(cells, chans)
                term = jnp.dot(w, k_ref[a * 3 + b], preferred_element_type=F32)
                total = term if total is None else total + term
        fld[...] = total.reshape(members, cols, chans)
        row = e * own_rows + i
        for blk in range(cols // 16):
            for lane in range(chans // 128):
                ln = pl.ds(lane * 128, 128)
                at = pl.ds(blk * 16, 16)
                tgt = t_ref[row, at, ln].astype(F32)
                f = [fld[m, at, ln] for m in range(members)]
                sums = [None] * members
                pair_w = None
                for m in range(members):
                    for o in range(m + 1, members):
                        sl, w = smooth(f[m] - f[o])
                        sums[m] = sl if sums[m] is None else sums[m] + sl
                        sums[o] = -sl if sums[o] is None else sums[o] - sl
                        pair_w = w if pair_w is None else pair_w + w
                own_w = None
                for m in range(members):
                    own_s, w = smooth(f[m] - tgt)
                    own_w = w if own_w is None else own_w + w
                    sl = own_s * (1.0 / members) - sums[m] * (1.0 / (members * (members - 1)))
                    sp[1, 1 + i, m, at, ln] = sl.astype(BF16)
                    if blk == 0:
                        eo[0, i, m : m + 1, ln] = sl[0:1]
                    if blk == cols // 16 - 1:
                        eo[1, i, m : m + 1, ln] = sl[15:16]
                loss_ref[:, ln] += own_w * (1.0 / members) - pair_w * (
                    1.0 / (members * (members - 1))
                )

        slt = sp[1, 1 + i].reshape(cells, chans).astype(F32).T.astype(BF16)
        for tap in range(9):
            a, b = tap // 3, tap % 3
            w = x_ref[b, i + a].reshape(cells, chans)
            p = jnp.dot(slt, w, preferred_element_type=F32)
            for dh in range(2):
                piece = tap * 2 + dh
                xh, off = piece // 9, (piece % 9) * 128
                for h in range(2):
                    acc[h, xh, off : off + 128] += p[
                        dh * 128 : dh * 128 + 128, h * 128 : h * 128 + 128
                    ]

    edges = [
        rcopy(eo.at[1], ei.at[0], s_e.at[0], r_e.at[0], right),
        rcopy(eo.at[0], ei.at[1], s_e.at[1], r_e.at[1], left),
    ]
    for c in edges:
        c.start()

    def span_of(p):
        return pl.ds(p * span, span)

    def part_of(p, i):
        return pl.ds(pl.multiple_of(p * span + i * part, 16), part)

    st_core = {}
    for p in range(PIECES):
        for j in range(2):
            h = 1 - xx if j == 0 else xx
            st_core[p, j] = rcopy(
                acc.at[1 - core, h, span_of(p)], r1.at[h, span_of(p)],
                s_st.at[p, j], r_st.at[p, j], cpeer,
            )
            st_core[p, j].start()
    total = loss_ref[...]
    total = total[0:8, 0:128] + total[8:16, 0:128] + total[0:8, 128:256] + total[8:16, 128:256]
    l1[...] = total
    ls_core = rcopy(l1, lr1, s_ls.at[0], r_ls.at[0], cpeer)
    ls_core.start()

    st_x = []
    for p in range(PIECES):
        st_core[p, 0].wait_recv()
        b2[span_of(p)] = (
            acc[core, 1 - xx, span_of(p)] + r1[1 - xx, span_of(p)]
        ).astype(BF16)
        st_x.append(rcopy(b2.at[span_of(p)], r2.at[span_of(p)], s_x2.at[p], r_x2.at[p], xpeer))
        st_x[p].start()
    ls_core.wait_recv()
    l2[...] = l1[...] + lr1[...]
    ls_x = rcopy(l2, lr2, s_ls.at[1], r_ls.at[1], xpeer)
    ls_x.start()

    for c in edges:
        c.wait_recv()

    @pl.loop(0, own_rows)
    def _(i):
        shift(sp, 1 + i, lambda side, mem: ei[side, i, mem : mem + 1])

    up = rcopy(
        sp.at[:, 1], sp.at[:, slots - 1], s_h.at[0], r_h.at[0], {"ens": jnp.maximum(e - 1, 0)}
    )
    down = rcopy(
        sp.at[:, slots - 2], sp.at[:, 0], s_h.at[1], r_h.at[1], {"ens": jnp.minimum(e + 1, 3)}
    )
    has_up, has_down = e > 0, e < 3

    @pl.when(has_up)
    def _():
        up.start()

    @pl.when(has_down)
    def _():
        down.start()

    def give(i, d, to, src):
        return rcopy(
            gib.at[i, pl.ds(to * mdev, mdev)], gi_ref.at[:, src * own_rows + i],
            s_g.at[d, i], r_g.at[src, i], {"ens": to},
        )

    def grad_in(start, stop):
        @pl.loop(start, stop)
        def _(i):
            total = None
            for a in range(3):
                for b in range(3):
                    w = sp[2 - b, i + 2 - a].reshape(cells, chans)
                    term = lax.dot_general(
                        w, k_ref[a * 3 + b], NT, preferred_element_type=F32
                    )
                    total = term if total is None else total + term
            gib[i] = total.reshape(members, cols, chans).astype(BF16)
            for d in (2, 3, 1):
                give(i, d, ens_at(d), e).start()
            for m in range(mdev):
                gi_ref[m, e * own_rows + i] = gib[i, e * mdev + m]

    def to_strip(p, d, i):
        peer = lax.rem(s + d, n)
        return rcopy(
            b3.at[part_of(p, peer)], r3.at[p, i], s_sp.at[p, d], r_sp.at[p, i], {"space": peer}
        )

    def loss_to_strip(d, i):
        return rcopy(l3, lr3.at[i], s_lp.at[d], r_lp.at[i], {"space": lax.rem(s + d, n)})

    def gather(p, d, i):
        return rcopy(
            gk_ref.at[core, xx, part_of(p, i)], gk_ref.at[core, xx, part_of(p, i)],
            s_ag.at[p, d], r_ag.at[p, i], {"space": lax.rem(s + d, n)},
        )

    marks = [1 + (own_rows - 2) * i // (2 * PIECES) for i in range(2 * PIECES + 1)]
    for p in range(PIECES):
        grad_in(marks[p], marks[p + 1])
        st_core[p, 1].wait_recv()
        st_x[p].wait_recv()
        total = acc[core, xx, span_of(p)] + r1[xx, span_of(p)] + r2[span_of(p)].astype(F32)
        r1[xx, span_of(p)] = total
        b3[span_of(p)] = total.astype(BF16)

        @pl.loop(1, n)
        def _(d):
            to_strip(p, d, s).start()

    ls_x.wait_recv()
    l3[...] = l2[...] + lr2[...]

    @pl.loop(1, n)
    def _(d):
        loss_to_strip(d, s).start()

    for p in range(PIECES):
        grad_in(marks[PIECES + p], marks[PIECES + p + 1])

        def take(d, g):
            peer = lax.rem(s + d, n)
            to_strip(p, d, peer).wait_recv()
            return g + r3[p, peer].astype(F32)

        total = lax.fori_loop(1, n, take, r1[xx, part_of(p, s)])
        gk_ref[core, xx, part_of(p, s)] = total.astype(BF16)

        @pl.loop(1, n)
        def _(d):
            gather(p, d, s).start()

    @pl.when(has_up)
    def _():
        up.wait_send()
        down.wait_recv()

    @pl.when(has_down)
    def _():
        down.wait_send()
        up.wait_recv()

    grad_in(0, 1)
    grad_in(own_rows - 1, own_rows)

    def take_loss(d, l):
        peer = lax.rem(s + d, n)
        loss_to_strip(d, peer).wait_recv()
        return l + lr3[peer]

    loss_ref[0:8, 0:128] = lax.fori_loop(1, n, take_loss, l3[...])

    ag_x, ag_c = [], []
    for p in range(PIECES):

        @pl.loop(1, n)
        def _(d):
            gather(p, d, lax.rem(s + d, n)).wait_recv()

        mine = gk_ref.at[core, xx, span_of(p)]
        ag_x.append(rcopy(mine, mine, s_ax.at[p], r_ax.at[p], xpeer))
        ag_x[p].start()
        ag_c.append(rcopy(mine, mine, s_ac.at[p, 0], r_ac.at[p, 0], cpeer))
        ag_c[-1].start()

    for p in range(PIECES):
        theirs = gk_ref.at[core, 1 - xx, span_of(p)]
        rcopy(theirs, theirs, s_ax.at[p], r_ax.at[p], xpeer).wait_recv()
        ag_c.append(rcopy(theirs, theirs, s_ac.at[p, 1], r_ac.at[p, 1], cpeer))
        ag_c[-1].start()

    for p in range(PIECES):
        for j in range(2):
            h = xx if j == 0 else 1 - xx
            theirs = gk_ref.at[1 - core, h, span_of(p)]
            rcopy(theirs, theirs, s_ac.at[p, j], r_ac.at[p, j], cpeer).wait_recv()

    @pl.loop(0, own_rows)
    def _(i):
        for d in range(1, 4):
            give(i, d, ens_at(d), e).wait_send()
            give(i, d, e, ens_at(d)).wait_recv()

    @pl.loop(0, slots)
    def _(slot):
        for d in range(1, 4):
            inside, c = row_of(d, ens_at(d), slot, e)

            @pl.when(inside)
            def _():
                c.wait_send()

    for d in range(4):
        for side in range(2):
            edge_of(side, d, e).wait_send()

    @pl.loop(1, n)
    def _(d):
        for p in range(PIECES):
            to_strip(p, d, s).wait_send()
            gather(p, d, s).wait_send()
        loss_to_strip(d, s).wait_send()

    for c in edges + list(st_core.values()) + st_x + [ls_core, ls_x] + ag_x + ag_c:
        c.wait_send()


def local(n, latents, targets, kernel):
    mdev, rows, cols, chans = latents.shape
    members = mdev * 4
    own_rows = rows // 4
    slots = own_rows + 2
    part = -(-9 * 128 // (16 * n * PIECES)) * 16
    hp = part * n * PIECES
    vmem, dma = pltpu.VMEM, pltpu.SemaphoreType.DMA
    shifted = vmem((3, slots, members, cols, chans), BF16)
    edge = vmem((2, own_rows, members, chans), F32)
    tile = vmem((8, 128), F32)
    gi, gk, loss = pl.pallas_call(
        functools.partial(body, n, members),
        name="crps_step",
        out_shape=(
            jax.ShapeDtypeStruct(latents.shape, BF16),
            jax.ShapeDtypeStruct((2, 2, hp, 128), BF16),
            jax.ShapeDtypeStruct((16, chans), F32),
        ),
        in_specs=[pl.BlockSpec(memory_space=vmem)] * 3,
        out_specs=(pl.BlockSpec(memory_space=vmem),) * 3,
        scratch_shapes=[
            shifted,
            vmem((2, rows + 2, mdev, chans), F32),
            vmem((2, 4, slots, mdev, chans), F32),
            vmem((members, cols, chans), F32),
            shifted,
            vmem((2, 2, hp, 128), F32),
            edge, edge,
            vmem((own_rows, members, cols, chans), BF16),
            vmem((2, hp, 128), F32),
            vmem((hp, 128), BF16),
            vmem((hp, 128), BF16),
            vmem((hp, 128), BF16),
            vmem((PIECES, n, part, 128), BF16),
            tile, tile, tile, tile, tile,
            vmem((n, 8, 128), F32),
            dma((4, slots)), dma((4, slots)), dma((2, 4)), dma((2, 4)), dma((2,)), dma((2,)),
            dma((2,)), dma((2,)), dma((4, own_rows)), dma((4, own_rows)),
            dma((PIECES, 2)), dma((PIECES, 2)), dma((PIECES,)), dma((PIECES,)),
            dma((2,)), dma((2,)), dma((PIECES, n)), dma((PIECES, n)), dma((n,)), dma((n,)),
            dma((PIECES, n)), dma((PIECES, n)),
            dma((PIECES,)), dma((PIECES,)), dma((PIECES, 2)), dma((PIECES, 2)),
        ],
        compiler_params=pltpu.CompilerParams(
            collective_id=0, has_side_effects=True, vmem_limit_bytes=48 * 2**20
        ),
    )(latents, targets, kernel.reshape(9, chans, chans))
    longitude = cols * n
    gk = gk[:, :, : 9 * 128].reshape(2, 9, chans, 128).transpose(1, 0, 3, 2)
    grad_kernel = gk.astype(F32).reshape(3, 3, chans, chans) / (members * rows * longitude)
    loss = jnp.sum(loss[0:8, 0:128]) / (rows * longitude * chans)
    return loss, gi, grad_kernel


def solution(mesh):
    in_specs = (P("ens", None, "space", None), P(None, "space", None), P())
    out_specs = (P(), P("ens", None, "space", None), P())
    return jax.shard_map(
        functools.partial(local, mesh.shape["space"]),
        mesh=mesh, in_specs=in_specs, out_specs=out_specs, check_vma=False,
    )
```

time: 79.6 us -> 77.4 us (0.972)
  Pallas kernels: 67.2 us -> 64.9 us
    pallas_call x1, Pallas kernels: 67.2 us -> 64.9 us  [local(): pl.pallas_call(functools.partial(body, n, members), name='crps_step', out...]
where the time goes in v3:
time: 77.4 us; the launch traced here: 77.1 us
  Pallas kernels  64.9 us (84%)
  local copies, waits for them, and re-layouts  7.54 us (10%)
  between operations  2.43 us (3%)
  other arithmetic  2.17 us (3%)
    pallas_call x1, Pallas kernels, local(): pl.pallas_call(functools.partial(body, n, members), name='crps_step', out...  64.9 us
    unnamed x7, local copies, waits for them, and re-layouts  4.5 us
    div x1, local copies, waits for them, and re-layouts, local(): gk.astype(F32).reshape(3, 3, chans, chans) / (members * rows * longitude)  3.04 us
    div x1, other arithmetic, local(): gk.astype(F32).reshape(3, 3, chans, chans) / (members * rows * longitude)  1.58 us

profile of v3, /device:TPU:1, one launch (start us, length us, event | category | flops | bytes accessed | tf_op | source)
XLA Modules:
  0.0 77.1 jit_solution(3086611642600388849)
XLA Ops:
  0.6 0.0 copy-start
  0.6 1.3 %copy-done = bf16[3,3,256,256]{3,2,1,0:T(8,128)(2,1)S(1)} copy-done((bf16[3,3,256,256]{3,2,1,0:T(8,128)(2,1)S(1)}, bf16[3,3,256,256]{3,2,1,0:T(8,128)(2,1)}, u32[]{:S(2)}) %copy-start) | copy-done | bytes 1179672
  1.9 0.0 copy-start.1
  1.9 1.2 %copy-done.1 = bf16[2,32,32,256]{3,2,1,0:T(8,128)(2,1)S(1)} copy-done((bf16[2,32,32,256]{3,2,1,0:T(8,128)(2,1)S(1)}, bf16[2,32,32,256]{3,2,1,0:T(8,128)(2,1)}, u32[]{:S(2)}) %copy-start.1) | copy-done | bytes 1048600
  3.1 0.0 copy-start.2
  3.1 1.0 %copy-done.2 = bf16[32,32,256]{2,1,0:T(8,128)(2,1)S(1)} copy-done((bf16[32,32,256]{2,1,0:T(8,128)(2,1)S(1)}, bf16[32,32,256]{2,1,0:T(8,128)(2,1)}, u32[]{:S(2)}) %copy-start.2) | copy-done | bytes 524312
  4.2 64.9 %crps_step.1 = (bf16[2,32,32,256]{3,2,1,0:T(8,128)(2,1)S(1)}, bf16[2,2,1152,128]{3,2,1,0:T(8,128)(2,1)S(1)}, f32[16,256]{1,0:T(8,128)S(1)}) custom-call(bf16[2,32,32,256]{3,2,1,0:T(8,128)(2,1)S(1)} %copy-done.1, bf16[32,32,256]{2,1,0:T(8,128)(2,1)S(1)} %copy-done.2, bf16[9,256,256]{2,1,0:T(8,128)(2,1)S(1)} %bitcast.5), custom_call_target="tpu_custom_call" | custom-call | tf_op jit(solution)/shard_map/crps_step/pallas_call | solution.py:430
  69.1 0.6 slice_reduce_fusion
  70.4 1.6 %convert_multiply_fusion = f32[2,2,1152,128]{3,2,1,0:T(8,128)} fusion(bf16[2,2,1152,128]{3,2,1,0:T(8,128)(2,1)S(1)} %get-tuple-element.8), kind=kLoop, calls=%fused_computation | loop fusion | flops 1179648 | bytes 3538944 | tf_op jit(solution)/shard_map/div | solution.py:469
  71.9 3.0 %copy.6 = f32[9,2,128,256]{3,2,1,0:T(8,128)} copy(f32[9,2,128,256]{2,3,0,1:T(8,128)} %bitcast.6) | data formatting | bytes 4718592 | tf_op jit(solution)/shard_map/div | solution.py:469
  75.0 1.0 %copy.8 = bf16[2,32,32,256]{3,2,1,0:T(8,128)(2,1)} copy(bf16[2,32,32,256]{3,2,1,0:T(8,128)(2,1)S(1)} %get-tuple-element.13) | data formatting | bytes 2097152
Async XLA Ops:
  0.6 1.3 %copy-start = (bf16[3,3,256,256]{3,2,1,0:T(8,128)(2,1)S(1)}, bf16[3,3,256,256]{3,2,1,0:T(8,128)(2,1)}, u32[]{:S(2)}) copy-start(bf16[3,3,256,256]{3,2,1,0:T(8,128)(2,1)} %param.5) | copy-start | bytes 3538948
  1.9 1.2 %copy-start.1 = (bf16[2,32,32,256]{3,2,1,0:T(8,128)(2,1)S(1)}, bf16[2,32,32,256]{3,2,1,0:T(8,128)(2,1)}, u32[]{:S(2)}) copy-start(bf16[2,32,32,256]{3,2,1,0:T(8,128)(2,1)} %lat_ref.1) | copy-start | bytes 3145732
  3.1 1.0 %copy-start.2 = (bf16[32,32,256]{2,1,0:T(8,128)(2,1)S(1)}, bf16[32,32,256]{2,1,0:T(8,128)(2,1)}, u32[]{:S(2)}) copy-start(bf16[32,32,256]{2,1,0:T(8,128)(2,1)} %t_ref.1) | copy-start | bytes 1572868

commit v4 on v3

--- a/solution.py
+++ b/solution.py
@@ -17,7 +17,7 @@
     n, members,
     lat_ref, t_ref, k_ref,
     gi_ref, gk_ref, loss_ref,
-    x_ref, leo, lei, fld, sp, acc, eo, ei, gib, r1, b2, r2, b3, r3, l1, lr1, l2, lr2, l3, lr3,
+    x_ref, leo, lei, fld, sp, acc, eo, ei, eh, gib, r1, b2, r2, b3, r3, l1, lr1, l2, lr2, l3, lr3,
     s_x, r_x, s_le, r_le, s_e, r_e, s_h, r_h, s_g, r_g,
     s_st, r_st, s_x2, r_x2, s_ls, r_ls, s_sp, r_sp, s_lp, r_lp,
     s_ag, r_ag, s_ax, r_ax, s_ac, r_ac,
@@ -252,21 +252,26 @@
     def _(i):
         shift(sp, 1 + i, lambda side, mem: ei[side, i, mem : mem + 1])
 
-    up = rcopy(
-        sp.at[:, 1], sp.at[:, slots - 1], s_h.at[0], r_h.at[0], {"ens": jnp.maximum(e - 1, 0)}
+    above, below = {"ens": jnp.maximum(e - 1, 0)}, {"ens": jnp.minimum(e + 1, 3)}
+    up = (
+        rcopy(sp.at[1, 1], sp.at[1, slots - 1], s_h.at[0], r_h.at[0], above),
+        rcopy(ei.at[:, 0], eh.at[1], s_h.at[2], r_h.at[2], above),
     )
-    down = rcopy(
-        sp.at[:, slots - 2], sp.at[:, 0], s_h.at[1], r_h.at[1], {"ens": jnp.minimum(e + 1, 3)}
+    down = (
+        rcopy(sp.at[1, slots - 2], sp.at[1, 0], s_h.at[1], r_h.at[1], below),
+        rcopy(ei.at[:, own_rows - 1], eh.at[0], s_h.at[3], r_h.at[3], below),
     )
     has_up, has_down = e > 0, e < 3
 
     @pl.when(has_up)
     def _():
-        up.start()
+        for c in up:
+            c.start()
 
     @pl.when(has_down)
     def _():
-        down.start()
+        for c in down:
+            c.start()
 
     def give(i, d, to, src):
         return rcopy(
@@ -343,13 +348,19 @@
 
     @pl.when(has_up)
     def _():
-        up.wait_send()
-        down.wait_recv()
+        for c in up:
+            c.wait_send()
+        for c in down:
+            c.wait_recv()
+        shift(sp, 0, lambda side, mem: eh[0, side, mem : mem + 1])
 
     @pl.when(has_down)
     def _():
-        down.wait_send()
-        up.wait_recv()
+        for c in down:
+            c.wait_send()
+        for c in up:
+            c.wait_recv()
+        shift(sp, slots - 1, lambda side, mem: eh[1, side, mem : mem + 1])
 
     grad_in(0, 1)
     grad_in(own_rows - 1, own_rows)
@@ -445,6 +456,7 @@
             shifted,
             vmem((2, 2, hp, 128), F32),
             edge, edge,
+            vmem((2, 2, members, chans), F32),
             vmem((own_rows, members, cols, chans), BF16),
             vmem((2, hp, 128), F32),
             vmem((hp, 128), BF16),
@@ -454,7 +466,7 @@
             tile, tile, tile, tile, tile,
             vmem((n, 8, 128), F32),
             dma((4, slots)), dma((4, slots)), dma((2, 4)), dma((2, 4)), dma((2,)), dma((2,)),
-            dma((2,)), dma((2,)), dma((4, own_rows)), dma((4, own_rows)),
+            dma((4,)), dma((4,)), dma((4, own_rows)), dma((4, own_rows)),
             dma((PIECES, 2)), dma((PIECES, 2)), dma((PIECES,)), dma((PIECES,)),
             dma((2,)), dma((2,)), dma((PIECES, n)), dma((PIECES, n)), dma((n,)), dma((n,)),
             dma((PIECES, n)), dma((PIECES, n)),

time: 77.4 us -> 74.8 us (0.966)
  Pallas kernels: 64.9 us -> 62.3 us
    pallas_call x1, Pallas kernels: 64.9 us -> 62.3 us  [local(): pl.pallas_call(functools.partial(body, n, members), name='crps_step', out...]
where the time goes in v4:
time: 74.8 us; the launch traced here: 74.5 us
  Pallas kernels  62.3 us (83%)
  local copies, waits for them, and re-layouts  7.54 us (10%)
  between operations  2.43 us (3%)
  other arithmetic  2.17 us (3%)
    pallas_call x1, Pallas kernels, local(): pl.pallas_call(functools.partial(body, n, members), name='crps_step', out...  62.3 us
    unnamed x7, local copies, waits for them, and re-layouts  4.5 us
    div x1, local copies, waits for them, and re-layouts, local(): gk.astype(F32).reshape(3, 3, chans, chans) / (members * rows * longitude)  3.04 us
    div x1, other arithmetic, local(): gk.astype(F32).reshape(3, 3, chans, chans) / (members * rows * longitude)  1.58 us

profile of v4, /device:TPU:1, one launch (start us, length us, event | category | flops | bytes accessed | tf_op | source)
XLA Modules:
  0.0 74.5 jit_solution(6410274398927667384)
XLA Ops:
  0.6 0.0 copy-start
  0.6 1.3 %copy-done = bf16[3,3,256,256]{3,2,1,0:T(8,128)(2,1)S(1)} copy-done((bf16[3,3,256,256]{3,2,1,0:T(8,128)(2,1)S(1)}, bf16[3,3,256,256]{3,2,1,0:T(8,128)(2,1)}, u32[]{:S(2)}) %copy-start) | copy-done | bytes 1179672
  1.9 0.0 copy-start.1
  1.9 1.2 %copy-done.1 = bf16[2,32,32,256]{3,2,1,0:T(8,128)(2,1)S(1)} copy-done((bf16[2,32,32,256]{3,2,1,0:T(8,128)(2,1)S(1)}, bf16[2,32,32,256]{3,2,1,0:T(8,128)(2,1)}, u32[]{:S(2)}) %copy-start.1) | copy-done | bytes 1048600
  3.1 0.0 copy-start.2
  3.1 1.0 %copy-done.2 = bf16[32,32,256]{2,1,0:T(8,128)(2,1)S(1)} copy-done((bf16[32,32,256]{2,1,0:T(8,128)(2,1)S(1)}, bf16[32,32,256]{2,1,0:T(8,128)(2,1)}, u32[]{:S(2)}) %copy-start.2) | copy-done | bytes 524312
  4.2 62.3 %crps_step.1 = (bf16[2,32,32,256]{3,2,1,0:T(8,128)(2,1)S(1)}, bf16[2,2,1152,128]{3,2,1,0:T(8,128)(2,1)S(1)}, f32[16,256]{1,0:T(8,128)S(1)}) custom-call(bf16[2,32,32,256]{3,2,1,0:T(8,128)(2,1)S(1)} %copy-done.1, bf16[32,32,256]{2,1,0:T(8,128)(2,1)S(1)} %copy-done.2, bf16[9,256,256]{2,1,0:T(8,128)(2,1)S(1)} %bitcast.5), custom_call_target="tpu_custom_call" | custom-call | tf_op jit(solution)/shard_map/crps_step/pallas_call | solution.py:441
  66.5 0.6 slice_reduce_fusion
  67.8 1.6 %convert_multiply_fusion = f32[2,2,1152,128]{3,2,1,0:T(8,128)} fusion(bf16[2,2,1152,128]{3,2,1,0:T(8,128)(2,1)S(1)} %get-tuple-element.8), kind=kLoop, calls=%fused_computation | loop fusion | flops 1179648 | bytes 3538944 | tf_op jit(solution)/shard_map/div | solution.py:481
  69.4 3.0 %copy.6 = f32[9,2,128,256]{3,2,1,0:T(8,128)} copy(f32[9,2,128,256]{2,3,0,1:T(8,128)} %bitcast.6) | data formatting | bytes 4718592 | tf_op jit(solution)/shard_map/div | solution.py:481
  72.4 1.0 %copy.8 = bf16[2,32,32,256]{3,2,1,0:T(8,128)(2,1)} copy(bf16[2,32,32,256]{3,2,1,0:T(8,128)(2,1)S(1)} %get-tuple-element.13) | data formatting | bytes 2097152
Async XLA Ops:
  0.6 1.3 %copy-start = (bf16[3,3,256,256]{3,2,1,0:T(8,128)(2,1)S(1)}, bf16[3,3,256,256]{3,2,1,0:T(8,128)(2,1)}, u32[]{:S(2)}) copy-start(bf16[3,3,256,256]{3,2,1,0:T(8,128)(2,1)} %param.5) | copy-start | bytes 3538948
  1.9 1.2 %copy-start.1 = (bf16[2,32,32,256]{3,2,1,0:T(8,128)(2,1)S(1)}, bf16[2,32,32,256]{3,2,1,0:T(8,128)(2,1)}, u32[]{:S(2)}) copy-start(bf16[2,32,32,256]{3,2,1,0:T(8,128)(2,1)} %lat_ref.1) | copy-start | bytes 3145732
  3.1 1.0 %copy-start.2 = (bf16[32,32,256]{2,1,0:T(8,128)(2,1)S(1)}, bf16[32,32,256]{2,1,0:T(8,128)(2,1)}, u32[]{:S(2)}) copy-start(bf16[32,32,256]{2,1,0:T(8,128)(2,1)} %t_ref.1) | copy-start | bytes 1572868
